TPU v7x, 32 devices: a whole 2x2x4 slice. The times are simulated.
32 devices in a mesh: depth: 2 (over y), row: 4 (over x, core), col: 4 (over z).
Axes of the slice: x: 2, y: 2, z: 4, core: 2. Of those that a mesh axis runs over, the one named last changes fastest.
Arguments:
- volume: float32 [2, 1024, 1024], P('depth', 'row', 'col'), may hold values from -6 to 6
- psf_spec: float32 [2, 2, 1024, 1024], P(None, 'depth', 'row', 'col'), may hold values from -1.5 to 1.5
- measured: float32 [1024, 1024], P('row', 'col'), may hold values from -6 to 6
- dual: float32 [3, 2, 1024, 1024], P(None, 'depth', 'row', 'col'), may hold values from -3 to 3
Outputs:
- updated: float32 [2, 1024, 1024], P('depth', 'row', 'col')
- shrunk: float32 [3, 2, 1024, 1024], P(None, 'depth', 'row', 'col')
- dual_next: float32 [3, 2, 1024, 1024], P(None, 'depth', 'row', 'col')
All inputs are finite; a program needn't handle non-finite values.
Results may differ from a plain program's by a relative error of at most 0.00005.
Values sent between devices are 32-bit elements; how exact they have to be, the bound alone decides.
A program may use at most 64 MiB of HBM per device.

v0:
```python
import math

import jax
import jax.numpy as jnp
from jax import lax
from jax.sharding import PartitionSpec as P

step_size = 1.0
shrink_level = 0.5
highest = lax.Precision.HIGHEST


def shifted(array, axis, by):
    length = lax.axis_size(axis)
    pairs = [(i, i + by) for i in range(length) if 0 <= i + by < length]
    return lax.ppermute(array, axis, pairs)


def twiddle(first_index, second_index, length, orient):
    phases = first_index[:, None] * second_index[None, :] % length
    angles = phases.astype(jnp.float32) * (orient * 2.0 * math.pi / length)
    return (jnp.cos(angles), jnp.sin(angles))


def complex_mix(field, apply_cos, apply_sin, keep):
    if field.shape[0] == 1:
        real_part = apply_cos(field[0])
        imag_part = apply_sin(field[0])
        return jnp.stack([real_part, imag_part])
    real_part = apply_cos(field[0]) - apply_sin(field[1])
    if keep == 1:
        return real_part[None]
    imag_part = apply_sin(field[0]) + apply_cos(field[1])
    return jnp.stack([real_part, imag_part])


def right_mult(field, cosines, sine_part, keep):

    def apply_cos(part):
        return jnp.dot(part, cosines, precision=highest, preferred_element_type=jnp.float32)

    def apply_sin(part):
        return jnp.dot(part, sine_part, precision=highest, preferred_element_type=jnp.float32)

    return complex_mix(field, apply_cos, apply_sin, keep)


def left_mult(cosines, sine_part, field, keep):

    def apply_cos(part):
        return jnp.einsum(
            "kh,phw->pkw", cosines, part, precision=highest, preferred_element_type=jnp.float32
        )

    def apply_sin(part):
        return jnp.einsum(
            "kh,phw->pkw", sine_part, part, precision=highest, preferred_element_type=jnp.float32
        )

    return complex_mix(field, apply_cos, apply_sin, keep)


def out_parts(field, keep):
    if field.shape[0] == 1:
        return 2
    return keep


def along_columns(field, orient, factor, keep):
    col_block = field.shape[3]
    width_all = col_block * lax.axis_size("col")
    parts_out = out_parts(field, keep)
    targets = lax.axis_index("col") * col_block + jnp.arange(col_block, dtype=jnp.int32)

    def accumulate(running, portion, offset):
        sources = jnp.arange(portion.shape[3], dtype=jnp.int32)
        cosines, sine_part = twiddle(sources, targets, width_all, orient)
        return right_mult(portion, cosines, sine_part, keep)

    start_value = jnp.zeros((parts_out,) + field.shape[1:], jnp.float32)
    result = (
        accumulate(start_value, lax.all_gather(field, "col", axis=3, tiled=True), jnp.int32(0))
        * factor
    )
    return result


def along_rows(field, orient, factor, keep):
    row_block = field.shape[2]
    height_all = row_block * lax.axis_size("row")
    parts_out = out_parts(field, keep)
    targets = lax.axis_index("row") * row_block + jnp.arange(row_block, dtype=jnp.int32)

    def accumulate(running, portion, offset):
        sources = jnp.arange(portion.shape[2], dtype=jnp.int32)
        cosines, sine_part = twiddle(targets, sources, height_all, orient)
        return left_mult(cosines, sine_part, portion, keep)

    start_value = jnp.zeros((parts_out,) + field.shape[1:], jnp.float32)
    result = (
        accumulate(start_value, lax.all_gather(field, "row", axis=2, tiled=True), jnp.int32(0))
        * factor
    )
    return result


def shards(volume, psf_spec, measured, dual):
    planes, row_block, col_block = volume.shape
    height_all = row_block * lax.axis_size("row")
    width_all = col_block * lax.axis_size("col")
    spectra = along_rows(along_columns(volume[None], -1.0, 1.0, 2), -1.0, 1.0, 2)
    kernel_real = psf_spec[0]
    kernel_imag = psf_spec[1]
    prod_real = jnp.sum(kernel_real * spectra[0] - kernel_imag * spectra[1], axis=0, keepdims=True)
    prod_imag = jnp.sum(kernel_real * spectra[1] + kernel_imag * spectra[0], axis=0, keepdims=True)
    local_sum = jnp.stack([prod_real, prod_imag])
    row_global = lax.axis_index("row") * row_block + jnp.arange(row_block, dtype=jnp.int32)
    col_global = lax.axis_index("col") * col_block + jnp.arange(col_block, dtype=jnp.int32)
    inside = ((row_global >= height_all // 4) & (row_global < 3 * height_all // 4))[:, None] & (
        (col_global >= width_all // 4) & (col_global < 3 * width_all // 4)
    )[None, :]
    empty_part = jnp.zeros_like(measured)
    summed_image = lax.psum(local_sum, "depth")
    sensor_image = along_columns(
        along_rows(summed_image, 1.0, 1.0 / height_all, 2), 1.0, 1.0 / width_all, 1
    )[0, 0]
    residual_map = jnp.where(inside, sensor_image - measured, empty_part)
    residual_spec = along_rows(along_columns(residual_map[None, None], -1.0, 1.0, 2), -1.0, 1.0, 2)
    back_real = kernel_real * residual_spec[0] + kernel_imag * residual_spec[1]
    back_imag = kernel_real * residual_spec[1] - kernel_imag * residual_spec[0]
    adjoint = along_columns(
        along_rows(jnp.stack([back_real, back_imag]), 1.0, 1.0 / height_all, 2),
        1.0,
        1.0 / width_all,
        1,
    )[0]
    updated = volume - step_size * adjoint
    plane_ahead = shifted(updated, "depth", -1)
    depth_count = planes * lax.axis_size("depth")
    plane_global = lax.axis_index("depth") * planes + jnp.arange(planes, dtype=jnp.int32)
    diff_depth = jnp.where(
        (plane_global < depth_count - 1)[:, None, None],
        jnp.concatenate([updated[1:], plane_ahead], axis=0) - updated,
        0.0,
    )
    row_ahead = shifted(updated[:, :1, :], "row", -1)
    diff_rows = jnp.where(
        (row_global < height_all - 1)[None, :, None],
        jnp.concatenate([updated[:, 1:, :], row_ahead], axis=1) - updated,
        0.0,
    )
    col_ahead = shifted(updated[:, :, :1], "col", -1)
    diff_cols = jnp.where(
        (col_global < width_all - 1)[None, None, :],
        jnp.concatenate([updated[:, :, 1:], col_ahead], axis=2) - updated,
        0.0,
    )
    combined = jnp.stack([diff_depth, diff_rows, diff_cols]) + dual
    dual_next = jnp.clip(combined, -shrink_level, shrink_level)
    return (updated, combined - dual_next, dual_next)


def solution(mesh):
    placed = (
        P("depth", "row", "col"),
        P(None, "depth", "row", "col"),
        P("row", "col"),
        P(None, "depth", "row", "col"),
    )
    return jax.shard_map(
        shards,
        mesh=mesh,
        in_specs=placed,
        out_specs=(
            P("depth", "row", "col"),
            P(None, "depth", "row", "col"),
            P(None, "depth", "row", "col"),
        ),
        check_vma=False,
    )
```

profile of v0, /device:TPU:0, one launch (start us, length us, event | category | flops | bytes accessed | tf_op | source)
XLA Modules:
  0.0 439.6 jit_solution(15999376654098091278)
XLA Ops:
  8.0 32.3 %all-gather.23.cloned.1.call-done = f32[1,256,1024]{2,1,0:T(8,128)} async-done(((f32[1,256,256]{2,1,0:T(8,128)}), f32[1,256,1024]{2,1,0:T(8,128)}) %all-gather.23.cloned.1.call-update) | async-done | bytes 1048592 | tf_op jit(solution)/shard_map/all_gather | solution.py:82
  40.3 6.9 %convolution_bitcast_fusion.2 = f32[1,1,256,256]{2,3,1,0:T(8,128)S(1)} fusion(f32[1,256,1024]{2,1,0:T(8,128)} %all-gather.23.cloned.1.call-done, s32[256]{0:T(256)S(1)} %iota_add_fusion), kind=kOutput, calls=%fused_computation.31 | convolution fusion | flops 808976384 | bytes 1311744 | tf_op jit(solution)/shard_map/dot_general | solution.py:43
  47.2 5.6 %convolution_bitcast_fusion.3 = f32[1,1,256,256]{2,3,1,0:T(8,128)S(1)} fusion(f32[1,256,1024]{2,1,0:T(8,128)S(1)} %copy-done.10, s32[256]{0:T(256)S(1)} %iota_add_fusion), kind=kOutput, calls=%fused_computation.32 | convolution fusion | flops 808976384 | bytes 1311744 | tf_op jit(solution)/shard_map/dot_general | solution.py:40
  54.2 21.5 %all-gather.11.cloned.1.call-done = f32[2,1,1024,256]{2,3,1,0:T(8,128)} async-done(((f32[2,1,256,256]{2,3,1,0:T(8,128)}), f32[2,1,1024,256]{2,3,1,0:T(8,128)}) %all-gather.11.cloned.1.call-update) | async-done | bytes 2097168 | tf_op jit(solution)/shard_map/all_gather | solution.py:101
  75.7 6.3 %fusion.28 = f32[256,256]{1,0:T(8,128)S(1)} fusion(f32[2,1,1024,256]{2,3,1,0:T(8,128)} %all-gather.11.cloned.1.call-done, s32[256]{0:T(256)S(1)} %iota_add_fusion.1), kind=kOutput, calls=%fused_computation.60 | convolution fusion | flops 808976384 | bytes 1311744 | tf_op jit(solution)/shard_map/kh,phw->pkw/dot_general | solution.py:56
  82.0 4.9 %fusion.29 = f32[256,256]{1,0:T(8,128)S(1)} fusion(f32[2,1,1024,256]{2,3,1,0:T(8,128)S(1)} %copy-done.4, s32[256]{0:T(256)S(1)} %iota_add_fusion.1), kind=kOutput, calls=%fused_computation.61 | convolution fusion | flops 808976384 | bytes 1311744 | tf_op jit(solution)/shard_map/kh,phw->pkw/dot_general | solution.py:51
  86.9 5.3 %fusion.11 = f32[1,256,256]{1,2,0:T(8,128)S(1)} fusion(f32[256,256]{1,0:T(8,128)S(1)} %fusion.28, f32[2,1,1024,256]{2,3,1,0:T(8,128)S(1)} %copy-done.4, s32[256]{0:T(256)S(1)} %iota_add_fusion.1), kind=kOutput, calls=%fused_computation.28 | convolution fusion | flops 809041920 | bytes 1573888 | tf_op jit(solution)/shard_map/kh,phw->pkw/dot_general | solution.py:51
  92.2 4.9 %fusion.89 = (f32[1,1,256,256]{2,3,1,0:T(8,128)S(1)}, f32[1,1,256,256]{2,3,1,0:T(8,128)S(1)}) fusion(f32[1,256,256]{1,2,0:T(8,128)S(1)} %fusion.11, f32[1,1,256,256]{2,3,1,0:T(8,128)S(1)} %copy.10, f32[1,1,256,256]{2,3,1,0:T(8,128)S(1)} %copy.9, f32[256,256]{1,0:T(8,128)S(1)} %fusion.29, s32[256]{0:T(256)S(1)} %iota_add_fusion.1, ...), kind=kOutput, calls=%fused_computation.119 | convolution fusion | flops 809435136 | bytes 2622464 | tf_op jit(solution)/shard_map/kh,phw->pkw/dot_general | solution.py:56
  98.1 28.8 %all-reduce.2.cloned.1.call-done = f32[2,1,256,256]{2,3,1,0:T(8,128)} async-done(((f32[2,1,256,256]{2,3,1,0:T(8,128)}), f32[2,1,256,256]{2,3,1,0:T(8,128)}) %all-reduce.2.cloned.1.call-update) | async-done | bytes 524304 | tf_op jit(solution)/shard_map/psum | solution.py:123
  127.1 23.8 %all-gather.13.cloned.1.call-done = f32[2,1,1024,256]{2,3,1,0:T(8,128)} async-done(((f32[2,1,256,256]{2,3,1,0:T(8,128)}), f32[2,1,1024,256]{2,3,1,0:T(8,128)}) %all-gather.13.cloned.1.call-update) | async-done | bytes 2097168 | tf_op jit(solution)/shard_map/all_gather | solution.py:101
  150.9 6.3 %fusion.30 = f32[256,256]{1,0:T(8,128)S(1)} fusion(f32[2,1,1024,256]{2,3,1,0:T(8,128)} %all-gather.13.cloned.1.call-done, s32[256]{0:T(256)S(1)} %iota_add_fusion.1), kind=kOutput, calls=%fused_computation.62 | convolution fusion | flops 808976384 | bytes 1311744 | tf_op jit(solution)/shard_map/kh,phw->pkw/dot_general | solution.py:56
  157.2 4.9 %fusion.31 = f32[256,256]{1,0:T(8,128)S(1)} fusion(f32[2,1,1024,256]{2,3,1,0:T(8,128)S(1)} %copy-done.8, s32[256]{0:T(256)S(1)} %iota_add_fusion.1), kind=kOutput, calls=%fused_computation.63 | convolution fusion | flops 808976384 | bytes 1311744 | tf_op jit(solution)/shard_map/kh,phw->pkw/dot_general | solution.py:51
  162.1 5.1 %fusion.9 = f32[1,1,256,256]{2,3,1,0:T(8,128)S(1)} fusion(f32[256,256]{1,0:T(8,128)S(1)} %fusion.30, f32[2,1,1024,256]{2,3,1,0:T(8,128)S(1)} %copy-done.8, s32[256]{0:T(256)S(1)} %iota_add_fusion.1), kind=kOutput, calls=%fused_computation.24 | convolution fusion | flops 809041920 | bytes 1573888 | tf_op jit(solution)/shard_map/kh,phw->pkw/dot_general | solution.py:51
  167.2 4.9 %fusion.10 = f32[1,1,256,256]{2,3,1,0:T(8,128)S(1)} fusion(f32[256,256]{1,0:T(8,128)S(1)} %fusion.31, f32[2,1,1024,256]{2,3,1,0:T(8,128)S(1)} %copy-done.8, s32[256]{0:T(256)S(1)} %iota_add_fusion.1), kind=kOutput, calls=%fused_computation.26 | convolution fusion | flops 809041920 | bytes 1573888 | tf_op jit(solution)/shard_map/kh,phw->pkw/dot_general | solution.py:56
  173.5 45.3 %all-gather.15.cloned.1.call-done = f32[2,1,256,1024]{2,3,1,0:T(8,128)} async-done(((f32[2,1,256,256]{2,3,1,0:T(8,128)}), f32[2,1,256,1024]{2,3,1,0:T(8,128)}) %all-gather.15.cloned.1.call-update) | async-done | bytes 2097168 | tf_op jit(solution)/shard_map/all_gather | solution.py:82
  218.8 6.9 %fusion.19 = f32[256,256]{1,0:T(8,128)S(1)} fusion(f32[2,1,256,1024]{2,3,1,0:T(8,128)} %all-gather.15.cloned.1.call-done, s32[256]{0:T(256)S(1)} %iota_add_fusion), kind=kOutput, calls=%fused_computation.47 | convolution fusion | flops 808976384 | bytes 1311744 | tf_op jit(solution)/shard_map/dot_general | solution.py:40
  225.7 6.3 %fusion.8 = f32[256,256]{1,0:T(8,128)} fusion(f32[256,256]{1,0:T(8,128)S(1)} %copy-done.12, f32[256,256]{1,0:T(8,128)S(1)} %fusion.19, f32[2,1,256,1024]{2,3,1,0:T(8,128)S(1)} %copy-done.6, s32[256]{0:T(256)S(1)} %iota_add_fusion, pred[256]{0:T(512)(128)(4,1)S(1)} %get-tuple-element.14, pred[256]{0:T(512)(128)(4,1)S(1)} %get-tuple-element.15), kind=kOutput, calls=%fused_computation.22 | convolution fusion | flops 809304064 | bytes 1837056 | tf_op jit(solution)/shard_map/dot_general | solution.py:43
  232.2 26.7 %all-gather.25.cloned.1.call-done = f32[256,1024]{1,0:T(8,128)} async-done(((f32[256,256]{1,0:T(8,128)}), f32[256,1024]{1,0:T(8,128)}) %all-gather.25.cloned.1.call-update) | async-done | bytes 1048592 | tf_op jit(solution)/shard_map/all_gather | solution.py:82
  258.9 6.2 %convolution_bitcast_fusion = f32[1,1,256,256]{3,2,1,0:T(8,128)S(1)} fusion(f32[256,1024]{1,0:T(8,128)} %all-gather.25.cloned.1.call-done, s32[256]{0:T(256)S(1)} %iota_add_fusion), kind=kOutput, calls=%fused_computation.17 | convolution fusion | flops 808976384 | bytes 1311744 | tf_op jit(solution)/shard_map/dot_general | solution.py:43
  271.1 21.8 %all-gather.17.cloned.1.call-done = f32[2,1,1024,256]{3,2,1,0:T(8,128)} async-done(((f32[2,1,256,256]{3,2,1,0:T(8,128)}), f32[2,1,1024,256]{3,2,1,0:T(8,128)}) %all-gather.17.cloned.1.call-update) | async-done | bytes 2097168 | tf_op jit(solution)/shard_map/all_gather | solution.py:101
  292.9 6.9 %fusion.32 = f32[256,256]{1,0:T(8,128)S(1)} fusion(f32[2,1,1024,256]{3,2,1,0:T(8,128)} %all-gather.17.cloned.1.call-done, s32[256]{0:T(256)S(1)} %iota_add_fusion.1), kind=kOutput, calls=%fused_computation.64 | convolution fusion | flops 808976384 | bytes 1311744 | tf_op jit(solution)/shard_map/kh,phw->pkw/dot_general | solution.py:56
  299.9 5.6 %fusion.33 = f32[256,256]{1,0:T(8,128)S(1)} fusion(f32[2,1,1024,256]{3,2,1,0:T(8,128)S(1)} %copy-done.5, s32[256]{0:T(256)S(1)} %iota_add_fusion.1), kind=kOutput, calls=%fused_computation.65 | convolution fusion | flops 808976384 | bytes 1311744 | tf_op jit(solution)/shard_map/kh,phw->pkw/dot_general | solution.py:51
  305.4 6.0 %fusion.4 = f32[1,256,256]{1,2,0:T(8,128)S(1)} fusion(f32[256,256]{1,0:T(8,128)S(1)} %fusion.32, f32[2,1,1024,256]{3,2,1,0:T(8,128)S(1)} %copy-done.5, s32[256]{0:T(256)S(1)} %iota_add_fusion.1), kind=kOutput, calls=%fused_computation.14 | convolution fusion | flops 809041920 | bytes 1573888 | tf_op jit(solution)/shard_map/kh,phw->pkw/dot_general | solution.py:51
  311.4 5.6 %fusion.93 = (f32[1,1,256,256]{2,3,1,0:T(8,128)S(1)}, f32[1,1,256,256]{2,3,1,0:T(8,128)S(1)}) fusion(f32[1,256,256]{1,2,0:T(8,128)S(1)} %fusion.4, f32[1,1,256,256]{2,3,1,0:T(8,128)S(1)} %copy.10, f32[1,1,256,256]{2,3,1,0:T(8,128)S(1)} %copy.9, f32[256,256]{1,0:T(8,128)S(1)} %fusion.33, s32[256]{0:T(256)S(1)} %iota_add_fusion.1, ...), kind=kOutput, calls=%fused_computation.123 | convolution fusion | flops 809435136 | bytes 2622464 | tf_op jit(solution)/shard_map/kh,phw->pkw/dot_general | solution.py:56
  318.1 22.5 %all-gather.19.cloned.1.call-done = f32[2,1,1024,256]{2,3,1,0:T(8,128)} async-done(((f32[2,1,256,256]{2,3,1,0:T(8,128)}), f32[2,1,1024,256]{2,3,1,0:T(8,128)}) %all-gather.19.cloned.1.call-update) | async-done | bytes 2097168 | tf_op jit(solution)/shard_map/all_gather | solution.py:101
  340.6 6.3 %fusion.34 = f32[256,256]{1,0:T(8,128)S(1)} fusion(f32[2,1,1024,256]{2,3,1,0:T(8,128)} %all-gather.19.cloned.1.call-done, s32[256]{0:T(256)S(1)} %iota_add_fusion.1), kind=kOutput, calls=%fused_computation.66 | convolution fusion | flops 808976384 | bytes 1311744 | tf_op jit(solution)/shard_map/kh,phw->pkw/dot_general | solution.py:56
  346.9 4.9 %fusion.35 = f32[256,256]{1,0:T(8,128)S(1)} fusion(f32[2,1,1024,256]{2,3,1,0:T(8,128)S(1)} %copy-done.7, s32[256]{0:T(256)S(1)} %iota_add_fusion.1), kind=kOutput, calls=%fused_computation.67 | convolution fusion | flops 808976384 | bytes 1311744 | tf_op jit(solution)/shard_map/kh,phw->pkw/dot_general | solution.py:51
  351.8 5.1 %fusion.2 = f32[1,1,256,256]{2,3,1,0:T(8,128)S(1)} fusion(f32[256,256]{1,0:T(8,128)S(1)} %fusion.34, f32[2,1,1024,256]{2,3,1,0:T(8,128)S(1)} %copy-done.7, s32[256]{0:T(256)S(1)} %iota_add_fusion.1), kind=kOutput, calls=%fused_computation.10 | convolution fusion | flops 809041920 | bytes 1573888 | tf_op jit(solution)/shard_map/kh,phw->pkw/dot_general | solution.py:51
  356.9 4.9 %fusion.3 = f32[1,1,256,256]{2,3,1,0:T(8,128)S(1)} fusion(f32[256,256]{1,0:T(8,128)S(1)} %fusion.35, f32[2,1,1024,256]{2,3,1,0:T(8,128)S(1)} %copy-done.7, s32[256]{0:T(256)S(1)} %iota_add_fusion.1), kind=kOutput, calls=%fused_computation.12 | convolution fusion | flops 809041920 | bytes 1573888 | tf_op jit(solution)/shard_map/kh,phw->pkw/dot_general | solution.py:56
  362.7 45.8 %all-gather.21.cloned.1.call-done = f32[2,1,256,1024]{2,3,1,0:T(8,128)} async-done(((f32[2,1,256,256]{2,3,1,0:T(8,128)}), f32[2,1,256,1024]{2,3,1,0:T(8,128)}) %all-gather.21.cloned.1.call-update) | async-done | bytes 2097168 | tf_op jit(solution)/shard_map/all_gather | solution.py:82
  408.5 7.1 %fusion.18 = f32[256,256]{1,0:T(8,128)S(1)} fusion(f32[2,1,256,1024]{2,3,1,0:T(8,128)} %all-gather.21.cloned.1.call-done, s32[256]{0:T(256)S(1)} %iota_add_fusion), kind=kOutput, calls=%fused_computation.40 | convolution fusion | flops 808976384 | bytes 1311744 | tf_op jit(solution)/shard_map/dot_general | solution.py:40
  415.7 5.5 %fusion.13 = f32[1,256,256]{2,1,0:T(8,128)S(1)} fusion(f32[1,256,256]{2,1,0:T(8,128)S(1)} %copy-done.3, f32[256,256]{1,0:T(8,128)S(1)} %fusion.18, f32[2,1,256,1024]{2,3,1,0:T(8,128)S(1)} %copy-done.9, s32[256]{0:T(256)S(1)} %iota_add_fusion), kind=kOutput, calls=%fused_computation.33 | convolution fusion | flops 809172992 | bytes 1836032 | tf_op jit(solution)/shard_map/dot_general | solution.py:43
  (70 shorter events, 24.0 us)
Async XLA Ops:
  7.2 33.1 %all-gather.23.cloned.1.call-start = ((), (), s32[]{:S(2)}) async-start(), calls=%async_computation.7 | async-start | bytes 1310720 | tf_op jit(solution)/shard_map/all_gather | solution.py:82
  7.9 67.8 %all-gather.11.cloned.1.call-start = ((), (), s32[]{:S(2)}) async-start(), calls=%async_computation | async-start | bytes 2621440 | tf_op jit(solution)/shard_map/all_gather | solution.py:101
  40.3 6.9 %copy-start.10 = (f32[1,256,1024]{2,1,0:T(8,128)S(1)}, f32[1,256,1024]{2,1,0:T(8,128)}, u32[]{:S(2)}) copy-start(f32[1,256,1024]{2,1,0:T(8,128)} %all-gather.23.cloned.1.call-done) | copy-start | bytes 3145732
  47.2 6.7 %copy-start.2 = (f32[2,1,256,256]{3,2,1,0:T(8,128)S(1)}, f32[2,1,256,256]{3,2,1,0:T(8,128)}, u32[]{:S(2)}) copy-start(f32[2,1,256,256]{3,2,1,0:T(8,128)} %param.5) | copy-start | bytes 1572868
  53.6 73.2 %all-reduce.2.cloned.1.call-start = ((), (), s32[]{:S(2)}) async-start(), calls=%async_computation.1 | async-start | bytes 1048576 | tf_op jit(solution)/shard_map/psum | solution.py:123
  75.7 6.3 %copy-start.4 = (f32[2,1,1024,256]{2,3,1,0:T(8,128)S(1)}, f32[2,1,1024,256]{2,3,1,0:T(8,128)}, u32[]{:S(2)}) copy-start(f32[2,1,1024,256]{2,3,1,0:T(8,128)} %all-gather.11.cloned.1.call-done) | copy-start | bytes 6291460
  98.0 52.8 %all-gather.13.cloned.1.call-start = ((), (), s32[]{:S(2)}) async-start(), calls=%async_computation.2 | async-start | bytes 2621440 | tf_op jit(solution)/shard_map/all_gather | solution.py:101
  126.9 91.9 %all-gather.15.cloned.1.call-start = ((), (), s32[]{:S(2)}) async-start(), calls=%async_computation.3 | async-start | bytes 2621440 | tf_op jit(solution)/shard_map/all_gather | solution.py:82
  150.9 6.3 %copy-start.8 = (f32[2,1,1024,256]{2,3,1,0:T(8,128)S(1)}, f32[2,1,1024,256]{2,3,1,0:T(8,128)}, u32[]{:S(2)}) copy-start(f32[2,1,1024,256]{2,3,1,0:T(8,128)} %all-gather.13.cloned.1.call-done) | copy-start | bytes 6291460
  173.0 85.9 %all-gather.25.cloned.1.call-start = ((), (), s32[]{:S(2)}) async-start(), calls=%async_computation.8 | async-start | bytes 1310720 | tf_op jit(solution)/shard_map/all_gather | solution.py:82
  173.4 52.2 %copy-start.12 = (f32[256,256]{1,0:T(8,128)S(1)}, f32[256,256]{1,0:T(8,128)}, u32[]{:S(2)}) copy-start(f32[256,256]{1,0:T(8,128)} %param.6) | copy-start | bytes 786436
  218.8 6.9 %copy-start.6 = (f32[2,1,256,1024]{2,3,1,0:T(8,128)S(1)}, f32[2,1,256,1024]{2,3,1,0:T(8,128)}, u32[]{:S(2)}) copy-start(f32[2,1,256,1024]{2,3,1,0:T(8,128)} %all-gather.15.cloned.1.call-done) | copy-start | bytes 6291460
  232.0 60.9 %all-gather.17.cloned.1.call-start = ((), (), s32[]{:S(2)}) async-start(), calls=%async_computation.4 | async-start | bytes 2621440 | tf_op jit(solution)/shard_map/all_gather | solution.py:101
  258.9 6.2 %copy-start.11 = (f32[256,1024]{1,0:T(8,128)S(1)}, f32[256,1024]{1,0:T(8,128)}, u32[]{:S(2)}) copy-start(f32[256,1024]{1,0:T(8,128)} %all-gather.25.cloned.1.call-done) | copy-start | bytes 3145732
  270.8 69.7 %all-gather.19.cloned.1.call-start = ((), (), s32[]{:S(2)}) async-start(), calls=%async_computation.5 | async-start | bytes 2621440 | tf_op jit(solution)/shard_map/all_gather | solution.py:101
  292.9 7.0 %copy-start.5 = (f32[2,1,1024,256]{3,2,1,0:T(8,128)S(1)}, f32[2,1,1024,256]{3,2,1,0:T(8,128)}, u32[]{:S(2)}) copy-start(f32[2,1,1024,256]{3,2,1,0:T(8,128)} %all-gather.17.cloned.1.call-done) | copy-start | bytes 6291460
  317.9 90.6 %all-gather.21.cloned.1.call-start = ((), (), s32[]{:S(2)}) async-start(), calls=%async_computation.6 | async-start | bytes 2621440 | tf_op jit(solution)/shard_map/all_gather | solution.py:82
  340.6 6.3 %copy-start.7 = (f32[2,1,1024,256]{2,3,1,0:T(8,128)S(1)}, f32[2,1,1024,256]{2,3,1,0:T(8,128)}, u32[]{:S(2)}) copy-start(f32[2,1,1024,256]{2,3,1,0:T(8,128)} %all-gather.19.cloned.1.call-done) | copy-start | bytes 6291460
  362.7 53.0 %copy-start.3 = (f32[1,256,256]{2,1,0:T(8,128)S(1)}, f32[1,256,256]{2,1,0:T(8,128)}, u32[]{:S(2)}) copy-start(f32[1,256,256]{2,1,0:T(8,128)} %param.4) | copy-start | bytes 786436
  408.5 7.1 %copy-start.9 = (f32[2,1,256,1024]{2,3,1,0:T(8,128)S(1)}, f32[2,1,256,1024]{2,3,1,0:T(8,128)}, u32[]{:S(2)}) copy-start(f32[2,1,256,1024]{2,3,1,0:T(8,128)} %all-gather.21.cloned.1.call-done) | copy-start | bytes 6291460
  421.2 11.4 %copy-start = (f32[1,256,256]{2,1,0:T(8,128)}, f32[1,256,256]{2,1,0:T(8,128)S(1)}, u32[]{:S(2)}) copy-start(f32[1,256,256]{2,1,0:T(8,128)S(1)} %fusion.13) | copy-start | bytes 786436
  421.2 10.1 %copy-start.1 = (f32[3,1,256,256]{3,2,1,0:T(8,128)S(1)}, f32[3,1,256,256]{3,2,1,0:T(8,128)}, u32[]{:S(2)}) copy-start(f32[3,1,256,256]{3,2,1,0:T(8,128)} %param.7) | copy-start | bytes 2359300
  421.2 9.9 %collective-permute-start = (f32[1,256,256]{2,1,0:T(8,128)S(1)}, f32[1,256,256]{2,1,0:T(8,128)S(1)}, u32[]{:S(2)}, u32[]{:S(2)}) collective-permute-start(f32[1,256,256]{2,1,0:T(8,128)S(1)} %fusion.13), channel_id=1, source_target_pairs={{16,0},{17,1},{18,2},{19,3},{20,4},{21,5},{22,6},{23,7},{24,8},{25... | collective-permute-start | bytes 786440 | tf_op jit(solution)/shard_map/ppermute | solution.py:16
  422.7 7.0 %collective-permute-start.2 = (f32[1,256,1]{2,1,0:T(8,128)S(1)}, f32[1,256,1]{2,1,0:T(8,128)S(1)}, u32[]{:S(2)}, u32[]{:S(2)}) collective-permute-start(f32[1,256,1]{2,1,0:T(8,128)S(1)} %slice.95), channel_id=1, source_target_pairs={{1,0},{2,1},{3,2},{5,4},{6,5},{7,6},{9,8},{10,9},{11,10},{13,12},{... | collective-permute-start | bytes 3080 | tf_op jit(solution)/shard_map/ppermute | solution.py:16
  424.0 5.7 %collective-permute-start.1 = (f32[1,1,256]{2,1,0:T(1,128)S(1)}, f32[1,1,256]{2,1,0:T(1,128)S(1)}, u32[]{:S(2)}, u32[]{:S(2)}) collective-permute-start(f32[1,1,256]{2,1,0:T(1,128)S(1)} %slice.93), channel_id=1, source_target_pairs={{4,0},{8,4},{12,8},{5,1},{9,5},{13,9},{6,2},{10,6},{14,10},{7,3},{... | collective-permute-start | bytes 3080 | tf_op jit(solution)/shard_map/ppermute | solution.py:16
Sparse Core Ops, SparseCore 0:
  9.5 30.6 all-gather.22
  53.8 21.9 all-gather.10
  98.2 28.6 all-reduce.1
  128.3 22.5 all-gather.12
  173.1 45.6 all-gather.14
  232.1 26.7 all-gather.24
  270.9 21.9 all-gather.16
  318.0 22.5 all-gather.18
  362.8 45.6 all-gather.20
where the time goes:
time: 448 us; the launch traced here: 440 us
  waiting for transfers between devices  275 us (61%)
  matrix products  137 us (31%)
  between operations  14.7 us (3%)
  other arithmetic  6.46 us (1%)
  starting transfers between devices  5.72 us (1%)
    all_gather x4, waiting for transfers between devices, along_columns(): lax.all_gather(field, 'col', axis=3, tiled=True)  150 us
    all_gather x4, waiting for transfers between devices, along_rows(): lax.all_gather(field, 'row', axis=2, tiled=True)  89.6 us
    dot_general x8, matrix products, apply_sin(): jnp.einsum('kh,phw->pkw', sine_part, part, precision=highest, preferred_e...  46.2 us
    dot_general x8, matrix products, apply_cos(): jnp.einsum('kh,phw->pkw', cosines, part, precision=highest, preferred_ele...  41.7 us
    psum x1, waiting for transfers between devices, shards(): summed_image = lax.psum(local_sum, 'depth')  28.8 us
    dot_general x4, matrix products, apply_sin(): jnp.dot(part, sine_part, precision=highest, preferred_element_type=jnp.fl...  24.9 us
    dot_general x4, matrix products, apply_cos(): jnp.dot(part, cosines, precision=highest, preferred_element_type=jnp.floa...  24.4 us
  transfers between devices with their start and end apart: 12, of which 11 were waited for; matrix products, arithmetic and copies ran while one was open for 0% of the time, Pallas kernels for 0%

commit v1 on v0

v1 whole, which is shorter than its diff:
```python
import functools

import jax
import jax.numpy as jnp
import numpy as np
from jax import lax
from jax.experimental import pallas as pl
from jax.experimental.pallas import tpu as pltpu
from jax.sharding import PartitionSpec as P

step_size = 1.0
shrink_level = 0.5
MESH = pl.DeviceIdType.MESH
highest = lax.Precision.HIGHEST


def dot(a, b):
    return lax.dot_general(a, b, (((1,), (0,)), ((), ())), precision=highest, preferred_element_type=jnp.float32)


def dot_nt(a, b):
    return lax.dot_general(a, b, (((1,), (1,)), ((), ())), precision=highest, preferred_element_type=jnp.float32)


def root(count, n):
    value = np.exp(-2j * np.pi * (n % count) / count)
    real, imag = float(value.real), float(value.imag)
    real = round(real) if abs(real - round(real)) < 1e-12 else real
    imag = round(imag) if abs(imag - round(imag)) < 1e-12 else imag
    return float(real), float(imag)


def add_scaled(total, scale, value):
    if scale == 0.0:
        return total
    if total is None:
        return value if scale == 1.0 else (-value if scale == -1.0 else scale * value)
    if scale == 1.0:
        return total + value
    if scale == -1.0:
        return total - value
    return total + scale * value


def spin(u):
    half = u.shape[-1] // 2
    lane = lax.broadcasted_iota(jnp.int32, u.shape, u.ndim - 1)
    rolled = pltpu.roll(u, half, u.ndim - 1)
    return jnp.where(lane < half, -rolled, rolled)


def body(D, R, C, hb, wb,
         vol, psf, meas, dual, mat_w, mat_h, tw_w, tw_h,
         upd, shr, dnx,
         r_vol, k_send, k_recv, r_meas, s1, r1, s2, r2, s3, r3, s4, r4, s5, r5, ups, h_dep, h_row, h_col,
         sm_vol, sm_k, sm_meas, sm1, sm2s, sm2r, sm3s, sm3r, sm4, sm5, sm_h):
    H, W = R * hb, C * wb
    rows, q = hb // C, wb // R
    rs = rows // D
    lo, hi, lo_c, hi_c = R // 4, 3 * R // 4, C // 4, 3 * C // 4
    NR = hi - lo
    N, n16, NO = D * R * C, R * C, D * NR * C
    d, r, c = lax.axis_index("depth"), lax.axis_index("row"), lax.axis_index("col")
    me16 = r * C + c
    me = d * n16 + me16

    def ids(t):
        return {"depth": t // n16, "row": (t // C) % R, "col": t % C}

    barrier = pltpu.get_barrier_semaphore()

    def greet(o, _):
        pl.semaphore_signal(barrier, inc=1, device_id=ids(lax.rem(me + o, N)), device_id_type=MESH)
        return 0

    lax.fori_loop(1, N, greet, 0)

    def rc(src, dst, ss, rsm, dev):
        return pltpu.make_async_remote_copy(src_ref=src, dst_ref=dst, send_sem=ss, recv_sem=rsm, device_id=dev, device_id_type=MESH)

    def loop(lower, upper, f):
        def g(i, x):
            f(i)
            return x
        lax.fori_loop(lower, upper, g, 0)

    class A2A:
        def __init__(self, n, pos, dev, src, recv, sems):
            self.n, self.pos, self.dev, self.src, self.recv, self.sems = n, pos, dev, src, recv, sems

        def start(self):
            def go(o):
                t = lax.rem(self.pos + o, self.n)
                rc(self.src(t), self.recv.at[self.pos], self.sems.at[0, t], self.sems.at[1, self.pos], self.dev(t)).start()
            loop(1, self.n, go)

        def wait(self):
            def go(o):
                t = lax.rem(self.pos + o, self.n)
                rc(self.src(t), self.recv.at[t], self.sems.at[0, t], self.sems.at[1, t], self.dev(t)).wait()
            loop(1, self.n, go)

    col_dev = lambda t: {"col": t}
    row_dev = lambda t: {"row": t}
    all_dev = lambda t: {"row": t // C, "col": lax.rem(t, C)}

    x_vol = A2A(C, c, col_dev, lambda t: vol.at[t], r_vol, sm_vol)
    x_k = A2A(R, r, row_dev, lambda t: k_send.at[t], k_recv, sm_k)
    x_meas = A2A(C, c, col_dev, lambda t: meas.at[t, d], r_meas, sm_meas)
    x1 = A2A(n16, me16, all_dev, lambda t: s1.at[t], r1, sm1)
    x4 = A2A(n16, me16, all_dev, lambda t: s4.at[t], r4, sm4)
    x5 = A2A(C, c, col_dev, lambda t: s5.at[t], r5, sm5)

    pl.semaphore_wait(barrier, N - 1)
    x_vol.start()
    r_vol[c] = vol[c]

    kin = jnp.concatenate([psf[0], psf[1]], axis=1)
    i0 = lax.broadcasted_iota(jnp.int32, (2 * wb, 2 * wb), 0)
    i1 = lax.broadcasted_iota(jnp.int32, (2 * wb, 2 * wb), 1)
    target = (lax.rem(i1, 2 * q) // q) * wb + R * lax.rem(i1, q) + i1 // (2 * q)
    perm_c = jnp.where(i0 == target, 1.0, 0.0).astype(jnp.float32)
    j0 = lax.broadcasted_iota(jnp.int32, (hb, hb), 0)
    j1 = lax.broadcasted_iota(jnp.int32, (hb, hb), 1)
    t_rows = hb // R
    perm_r = jnp.where(j1 == R * lax.rem(j0, t_rows) + j0 // t_rows, 1.0, 0.0).astype(jnp.float32)
    kk = dot(perm_r, dot(kin, perm_c))
    for j in range(R):
        k_send[j] = kk[:, 2 * q * j:2 * q * (j + 1)]
    x_meas.start()
    r_meas[c] = meas[c, d]

    def fwd_w(blocks, first):
        tre, tim = [], []
        for k1 in range(C):
            yr = yi = None
            for i, blk in enumerate(blocks):
                a, b = root(C, (first + i) * k1)
                yr, yi = add_scaled(yr, a, blk), add_scaled(yi, b, blk)
            ct, st = tw_w[0, k1:k1 + 1, :], tw_w[1, k1:k1 + 1, :]
            if yi is None:
                tre.append(yr * ct)
                tim.append(yr * st)
            else:
                tre.append(yr * ct - yi * st)
                tim.append(yr * st + yi * ct)
        both = jnp.concatenate([jnp.concatenate(tre, 0), jnp.concatenate(tim, 0)], 1)
        return dot(both, mat_w[...])

    def inv_w(z, count, first, last):
        g = dot_nt(z, mat_w[...]) * (1.0 / W)
        gr, gi = [], []
        for k1 in range(C):
            a = g[k1 * count:(k1 + 1) * count, :wb]
            b = g[k1 * count:(k1 + 1) * count, wb:]
            ct, st = tw_w[0, k1:k1 + 1, :], tw_w[1, k1:k1 + 1, :]
            gr.append(a * ct + b * st)
            gi.append(b * ct - a * st)
        out = []
        for n1 in range(first, last):
            total = None
            for k1 in range(C):
                a, b = root(C, n1 * k1)
                total = add_scaled(total, a, gr[k1])
                total = add_scaled(total, b, gi[k1])
            out.append(total)
        return out

    def fwd_h(us, first):
        vs = [spin(u) for u in us]
        tu, tv = [], []
        for k1 in range(R):
            yu = yv = None
            for i in range(len(us)):
                a, b = root(R, (first + i) * k1)
                yu = add_scaled(add_scaled(yu, a, us[i]), b, vs[i])
                yv = add_scaled(add_scaled(yv, a, vs[i]), -b, us[i])
            ct, st = tw_h[:, k1:k1 + 1], tw_h[:, R + k1:R + k1 + 1]
            tu.append(yu * ct + yv * st)
            tv.append(yv * ct - yu * st)
        return dot(mat_h[0], jnp.concatenate(tu, 1)) + dot(mat_h[1], jnp.concatenate(tv, 1))

    def inv_h(ps, first, last):
        vs = [spin(p) for p in ps]
        g = (dot(mat_h[0], jnp.concatenate(ps, 1)) - dot(mat_h[1], jnp.concatenate(vs, 1))) * (1.0 / H)
        gu, gv = [], []
        for k1 in range(R):
            u = g[:, 2 * q * k1:2 * q * (k1 + 1)]
            v = spin(u)
            ct, st = tw_h[:, k1:k1 + 1], tw_h[:, R + k1:R + k1 + 1]
            gu.append(u * ct - v * st)
            gv.append(v * ct + u * st)
        out = []
        for n1 in range(first, last):
            total = None
            for k1 in range(R):
                a, b = root(R, n1 * k1)
                total = add_scaled(add_scaled(total, a, gu[k1]), -b, gv[k1])
            out.append(total)
        return out

    def kernel_parts(k1):
        k = jnp.concatenate([k_recv[j, k1 * t_rows:(k1 + 1) * t_rows, :] for j in range(R)], 0)
        rolled = pltpu.roll(k, q, 1)
        lane = lax.broadcasted_iota(jnp.int32, k.shape, 1)
        return jnp.where(lane < q, k, rolled), jnp.where(lane < q, rolled, k)

    x_vol.wait()
    z = fwd_w([r_vol[j] for j in range(C)], 0)
    for k1 in range(R):
        for j in range(C):
            s1[k1 * C + j] = z[k1 * rows:(k1 + 1) * rows, 2 * q * j:2 * q * (j + 1)]
    x1.start()
    x_k.start()
    r1[me16] = s1[me16]
    k_recv[r] = k_send[r]
    x1.wait()
    x_k.wait()

    def joined(ref, first, count):
        return jnp.concatenate([ref[first + j] for j in range(count)], 0)

    s = fwd_h([joined(r1, j * C, C) for j in range(R)], 0)
    ps = []
    for k1 in range(R):
        kr, ki = kernel_parts(k1)
        u = s[:, 2 * q * k1:2 * q * (k1 + 1)]
        ps.append(kr * u + ki * spin(u))
    xs = inv_h(ps, lo, hi)

    for i in range(NR):
        for j in range(C):
            for e in range(D):
                s2[(e * NR + i) * C + j] = xs[i][j * rows + e * rs:j * rows + (e + 1) * rs, :]

    def owner_id(t):
        return (t // (NR * C)) * n16 + (lo + (t // C) % NR) * C + t % C

    def send2(o):
        t = lax.rem(me + o, NO)
        w = owner_id(t)

        @pl.when(w != me)
        def _():
            rc(s2.at[t], r2.at[me], sm2s.at[t], sm2r.at[me], ids(w)).start()

        @pl.when(w == me)
        def _():
            r2[me] = s2[t]

    loop(0, NO, send2)
    x_meas.wait()
    is_owner = (r >= lo) & (r < hi)
    my_owner = ((r - lo) * C + c) * D + d

    @pl.when(is_owner)
    def _():
        def wait2(o):
            t = lax.rem(me + o, N)
            rc(r2.at[t], r2.at[t], sm2s.at[0], sm2r.at[t], ids(t)).wait_recv()

        loop(1, N, wait2)
        zs = []
        for k1 in range(R):
            pieces = []
            for j in range(C):
                total = r2[k1 * C + j]
                for e in range(1, D):
                    total = total + r2[e * n16 + k1 * C + j]
                pieces.append(total)
            zs.append(jnp.concatenate(pieces, 1))
        sensor = inv_w(jnp.concatenate(zs, 0), rs, lo_c, hi_c)
        res = [sensor[i] - r_meas[lo_c + i] for i in range(hi_c - lo_c)]
        zz = fwd_w(res, lo_c)
        for k1 in range(R):
            for j in range(C):
                s3[k1 * C + j] = zz[k1 * rs:(k1 + 1) * rs, 2 * q * j:2 * q * (j + 1)]

        def send3(o):
            t = lax.rem(me + o, N)
            rc(s3.at[lax.rem(t, n16)], r3.at[my_owner], sm3s.at[t], sm3r.at[my_owner], ids(t)).start()

        loop(1, N, send3)
        r3[my_owner] = s3[me16]

        def drain3(o):
            t = lax.rem(me + o, N)
            rc(s3.at[lax.rem(t, n16)], r3.at[my_owner], sm3s.at[t], sm3r.at[my_owner], ids(t)).wait_send()

        loop(1, N, drain3)

    def drain2(o):
        t = lax.rem(me + o, NO)
        w = owner_id(t)

        @pl.when(w != me)
        def _():
            rc(s2.at[t], r2.at[me], sm2s.at[t], sm2r.at[me], ids(w)).wait_send()

    loop(0, NO, drain2)

    def wait3(t):
        w = (t % D) * n16 + (lo + t // (C * D)) * C + (t // D) % C

        @pl.when(w != me)
        def _():
            rc(r3.at[t], r3.at[t], sm3s.at[0], sm3r.at[t], ids(w)).wait_recv()

    loop(0, NO, wait3)
    s = fwd_h([joined(r3, i * C * D, C * D) for i in range(NR)], lo)
    ps = []
    for k1 in range(R):
        kr, ki = kernel_parts(k1)
        u = s[:, 2 * q * k1:2 * q * (k1 + 1)]
        ps.append(kr * u - ki * spin(u))
    xs = inv_h(ps, 0, R)
    for i in range(R):
        for j in range(C):
            s4[i * C + j] = xs[i][j * rows:(j + 1) * rows, :]
    x4.start()
    r4[me16] = s4[me16]
    x4.wait()
    zs = [jnp.concatenate([r4[k1 * C + j] for j in range(C)], 1) for k1 in range(R)]
    adj = inv_w(jnp.concatenate(zs, 0), rows, 0, C)
    for j in range(C):
        s5[j] = adj[j]
    x5.start()
    r5[c] = s5[c]
    x5.wait()
    for j in range(C):
        ups[j * rows:(j + 1) * rows, :] = vol[j] - step_size * r5[j]

    down_d, down_r, down_c = lax.rem(d + D - 1, D), lax.rem(r + R - 1, R), lax.rem(c + C - 1, C)
    copies = [
        rc(ups.at[0:8, :], h_row, sm_h.at[0, 1], sm_h.at[1, 1], {"row": down_r}),
        rc(ups.at[:, 0:128], h_col, sm_h.at[0, 2], sm_h.at[1, 2], {"col": down_c}),
        rc(ups, h_dep, sm_h.at[0, 0], sm_h.at[1, 0], {"depth": down_d}),
    ]
    for cp in copies:
        cp.start()
    u = ups[...]
    upd[0] = u

    def finish(i, diff):
        combined = diff + dual[i, 0]
        clipped = jnp.clip(combined, -shrink_level, shrink_level)
        shr[i, 0] = combined - clipped
        dnx[i, 0] = clipped

    copies[0].wait()
    rid = lax.broadcasted_iota(jnp.int32, (hb, wb), 0)
    nxt = jnp.where(rid == hb - 1, jnp.broadcast_to(h_row[0:1, :], (hb, wb)), pltpu.roll(u, hb - 1, 0))
    finish(1, jnp.where(r * hb + rid < H - 1, nxt - u, 0.0))
    copies[1].wait()
    cid = lax.broadcasted_iota(jnp.int32, (hb, wb), 1)
    nxt = jnp.where(cid == wb - 1, jnp.broadcast_to(h_col[:, 0:1], (hb, wb)), pltpu.roll(u, wb - 1, 1))
    finish(2, jnp.where(c * wb + cid < W - 1, nxt - u, 0.0))
    copies[2].wait()
    live = (d + rid * 0) < D - 1
    finish(0, jnp.where(live, h_dep[...] - u, 0.0))


def shards(D, R, C, volume, psf_spec, measured, dual):
    planes, hb, wb = volume.shape
    assert planes == 1 and R == C
    H, W = hb * R, wb * C
    rows, q = hb // C, wb // R
    rs = rows // D
    NO, N, n16 = D * (3 * R // 4 - R // 4) * C, D * R * C, R * C
    n2, k2 = np.arange(wb), np.arange(wb)
    f = np.exp(-2j * np.pi * ((n2[:, None] * k2[None]) % wb) / wb).reshape(wb, C, 1, wb // C)
    top = np.concatenate([f.real, f.imag], 2).reshape(wb, 2 * wb)
    bot = np.concatenate([-f.imag, f.real], 2).reshape(wb, 2 * wb)
    mat_w = np.concatenate([top, bot], 0).astype(np.float32)
    m = np.arange(hb)
    g = np.exp(-2j * np.pi * ((m[:, None] * m[None]) % hb) / hb)
    mat_h = np.stack([g.real, g.imag]).astype(np.float32)
    t = np.exp(-2j * np.pi * (np.arange(C)[:, None] * n2[None]) / W)
    tw_w = np.stack([t.real, t.imag]).astype(np.float32)
    t = np.exp(-2j * np.pi * (m[:, None] * np.arange(R)[None]) / H)
    tw_h = np.concatenate([t.real, t.imag], 1).astype(np.float32)
    f32 = jnp.float32
    V = pltpu.VMEM
    dma = pltpu.SemaphoreType.DMA
    vm = pl.BlockSpec(memory_space=pltpu.VMEM)
    return pl.pallas_call(
        functools.partial(body, D, R, C, hb, wb),
        name="admm",
        out_shape=(
            jax.ShapeDtypeStruct((1, hb, wb), f32),
            jax.ShapeDtypeStruct((3, 1, hb, wb), f32),
            jax.ShapeDtypeStruct((3, 1, hb, wb), f32),
        ),
        in_specs=[vm] * 8,
        out_specs=(vm, vm, vm),
        scratch_shapes=[
            V((C, rows, wb), f32),
            V((R, hb, 2 * q), f32), V((R, hb, 2 * q), f32),
            V((C, rs, wb), f32),
            V((n16, rows, 2 * q), f32), V((n16, rows, 2 * q), f32),
            V((NO, rs, 2 * q), f32), V((N, rs, 2 * q), f32),
            V((n16, rs, 2 * q), f32), V((NO, rs, 2 * q), f32),
            V((n16, rows, 2 * q), f32), V((n16, rows, 2 * q), f32),
            V((C, rows, wb), f32), V((C, rows, wb), f32),
            V((hb, wb), f32), V((hb, wb), f32), V((8, wb), f32), V((hb, 128), f32),
            dma((2, C)), dma((2, R)), dma((2, C)), dma((2, n16)), dma((NO,)), dma((N,)),
            dma((N,)), dma((NO,)), dma((2, n16)), dma((2, C)), dma((2, 3)),
        ],
        compiler_params=pltpu.CompilerParams(
            collective_id=0, has_side_effects=True, vmem_limit_bytes=60 * 1024 * 1024
        ),
    )(
        volume.reshape(C, rows, wb), psf_spec.reshape(2, hb, wb), measured.reshape(C, D, rs, wb), dual,
        jnp.asarray(mat_w), jnp.asarray(mat_h), jnp.asarray(tw_w), jnp.asarray(tw_h),
    )


def solution(mesh):
    placed = (
        P("depth", "row", "col"),
        P(None, "depth", "row", "col"),
        P("row", "col"),
        P(None, "depth", "row", "col"),
    )
    return jax.shard_map(
        functools.partial(shards, mesh.shape["depth"], mesh.shape["row"], mesh.shape["col"]),
        mesh=mesh,
        in_specs=placed,
        out_specs=(
            P("depth", "row", "col"),
            P(None, "depth", "row", "col"),
            P(None, "depth", "row", "col"),
        ),
        check_vma=False,
    )
```

time: 448 us -> 88.8 us (0.20); the launches traced: 440 us -> 87.7 us
  waiting for transfers between devices: 275 us -> 0 us
  matrix products: 137 us -> 0 us
  Pallas kernels: 0 us -> 82.4 us
  between operations: 14.7 us -> 0.64 us
  other arithmetic: 6.46 us -> 0 us
  starting transfers between devices: 5.72 us -> 0 us
    all_gather x8 -> x0, waiting for transfers between devices: 240 us -> none  [the longest x4 150 us: along_columns(): lax.all_gather(field, 'col', axis=3, tiled=True)]
    dot_general x24 -> x0, matrix products: 137 us -> none  [the longest x8 46.2 us: apply_sin(): jnp.einsum('kh,phw->pkw', sine_part, part, precision=highest, preferred_e...]
    pallas_call x0 -> x1, Pallas kernels: none -> 82.4 us  [shards(): pl.pallas_call(functools.partial(body, D, R, C, hb, wb), name='admm', out...]
    psum x1 -> x0, waiting for transfers between devices: 28.8 us -> none  [shards(): summed_image = lax.psum(local_sum, 'depth')]
    ppermute x3 -> x0, waiting for transfers between devices: 5.66 us -> none  [shifted(): return lax.ppermute(array, axis, pairs)]
  transfers between devices with their start and end apart: 12 -> 0, of which waited for: 11 -> 0; matrix products, arithmetic and copies ran while one was open for 0% -> 0% of each run, Pallas kernels for 0% -> 0%
where the time goes in v1:
time: 88.8 us; the launch traced here: 87.7 us
  Pallas kernels  82.4 us (93%)
  local copies, waits for them, and re-layouts  4.69 us (5%)
    pallas_call x1, Pallas kernels, shards(): pl.pallas_call(functools.partial(body, D, R, C, hb, wb), name='admm', out...  82.4 us
    unnamed x5, local copies, waits for them, and re-layouts  4.69 us

profile of v1, /device:TPU:0, one launch (start us, length us, event | category | flops | bytes accessed | tf_op | source)
XLA Modules:
  0.0 87.7 jit_solution(17811089583861666454)
XLA Ops:
  0.6 82.4 %admm.1 = (f32[1,256,256]{2,1,0:T(8,128)}, f32[3,1,256,256]{3,2,1,0:T(8,128)}, f32[3,1,256,256]{3,2,1,0:T(8,128)}) custom-call(f32[4,64,256]{2,1,0:T(8,128)} %bitcast.4, f32[2,256,256]{2,1,0:T(8,128)} %bitcast.3, f32[4,2,32,256]{3,2,1,0:T(8,128)} %bitcast.5, f32[3,1,256,256]{3,2,1,0:T(8,128)} %dual.1, f32[512,512]{1,0:T(8,128)} %constant.8.clone.mat_w, ...), custom_call_target="tpu_custom_call" | custom-call | tf_op jit(solution)/shard_map/admm/pallas_call | solution.py:386
  83.0 1.7 %copy.14 = f32[1,256,256]{2,1,0:T(8,128)} copy(f32[1,256,256]{2,1,0:T(8,128)} %get-tuple-element.6) | data formatting | bytes 524288
  84.7 0.0 copy-start
  84.7 2.1 %copy.15 = f32[3,1,256,256]{3,2,1,0:T(8,128)} copy(f32[3,1,256,256]{3,2,1,0:T(8,128)} %get-tuple-element.7) | data formatting | bytes 1572864
  86.8 0.0 copy-done
  86.8 0.9 %copy.16 = f32[3,1,256,256]{3,2,1,0:T(8,128)} copy(f32[3,1,256,256]{3,2,1,0:T(8,128)S(1)} %copy-done) | data formatting | bytes 1572864
Async XLA Ops:
  84.7 2.1 %copy-start = (f32[3,1,256,256]{3,2,1,0:T(8,128)S(1)}, f32[3,1,256,256]{3,2,1,0:T(8,128)}, u32[]{:S(2)}) copy-start(f32[3,1,256,256]{3,2,1,0:T(8,128)} %get-tuple-element.8) | copy-start | bytes 2359300

commit v2 on v1

--- a/solution.py
+++ b/solution.py
@@ -11,15 +11,25 @@
 step_size = 1.0
 shrink_level = 0.5
 MESH = pl.DeviceIdType.MESH
-highest = lax.Precision.HIGHEST
-
-
-def dot(a, b):
-    return lax.dot_general(a, b, (((1,), (0,)), ((), ())), precision=highest, preferred_element_type=jnp.float32)
-
-
-def dot_nt(a, b):
-    return lax.dot_general(a, b, (((1,), (1,)), ((), ())), precision=highest, preferred_element_type=jnp.float32)
+
+
+def dot_of(a, b, side):
+    return lax.dot_general(a, b, (((1,), (side,)), ((), ())), preferred_element_type=jnp.float32)
+
+
+def halves(a):
+    high = a.astype(jnp.bfloat16)
+    return high, (a - high.astype(jnp.float32)).astype(jnp.bfloat16)
+
+
+def dot_right(a, table, side):
+    high, low = halves(a)
+    return dot_of(high, table[0], side) + (dot_of(high, table[1], side) + dot_of(low, table[0], side))
+
+
+def dot_left(table, b):
+    high, low = b
+    return dot_of(table[0], high, 0) + (dot_of(table[0], low, 0) + dot_of(table[1], high, 0))
 
 
 def root(count, n):
@@ -50,10 +60,10 @@
 
 
 def body(D, R, C, hb, wb,
-         vol, psf, meas, dual, mat_w, mat_h, tw_w, tw_h,
-         upd, shr, dnx,
-         r_vol, k_send, k_recv, r_meas, s1, r1, s2, r2, s3, r3, s4, r4, s5, r5, ups, h_dep, h_row, h_col,
-         sm_vol, sm_k, sm_meas, sm1, sm2s, sm2r, sm3s, sm3r, sm4, sm5, sm_h):
+         vol, psf, meas, mat_w, mat_h, tw_w, tw_h,
+         out_u, out_dep, out_row, out_col,
+         r_vol, k_send, k_recv, r_meas, s1, r1, s2, r2, s3, r3, s4, r4, s5, r5, ups, h_dep, h_row, h_col, edge,
+         sm_vol, sm_k, sm_meas, sm1, sm2s, sm2r, sm3s, sm3r, sm4, sm5, sm_h, sm_dep):
     H, W = R * hb, C * wb
     rows, q = hb // C, wb // R
     rs = rows // D
@@ -124,9 +134,14 @@
     j1 = lax.broadcasted_iota(jnp.int32, (hb, hb), 1)
     t_rows = hb // R
     perm_r = jnp.where(j1 == R * lax.rem(j0, t_rows) + j0 // t_rows, 1.0, 0.0).astype(jnp.float32)
-    kk = dot(perm_r, dot(kin, perm_c))
+    perm_c, perm_r = perm_c.astype(jnp.bfloat16), perm_r.astype(jnp.bfloat16)
+    kin_high, kin_low = halves(kin)
+    kk = (dot_of(perm_r, dot_of(kin_high, perm_c, 0).astype(jnp.bfloat16), 0)
+          + dot_of(perm_r, dot_of(kin_low, perm_c, 0).astype(jnp.bfloat16), 0))
     for j in range(R):
         k_send[j] = kk[:, 2 * q * j:2 * q * (j + 1)]
+    x_k.start()
+    k_recv[r] = k_send[r]
     x_meas.start()
     r_meas[c] = meas[c, d]
 
@@ -145,10 +160,10 @@
                 tre.append(yr * ct - yi * st)
                 tim.append(yr * st + yi * ct)
         both = jnp.concatenate([jnp.concatenate(tre, 0), jnp.concatenate(tim, 0)], 1)
-        return dot(both, mat_w[...])
+        return dot_right(both, (mat_w[0], mat_w[1]), 0)
 
     def inv_w(z, count, first, last):
-        g = dot_nt(z, mat_w[...]) * (1.0 / W)
+        g = dot_right(z, (mat_w[0], mat_w[1]), 1) * (1.0 / W)
         gr, gi = [], []
         for k1 in range(C):
             a = g[k1 * count:(k1 + 1) * count, :wb]
@@ -178,11 +193,13 @@
             ct, st = tw_h[:, k1:k1 + 1], tw_h[:, R + k1:R + k1 + 1]
             tu.append(yu * ct + yv * st)
             tv.append(yv * ct - yu * st)
-        return dot(mat_h[0], jnp.concatenate(tu, 1)) + dot(mat_h[1], jnp.concatenate(tv, 1))
+        return (dot_left((mat_h[0, 0], mat_h[1, 0]), halves(jnp.concatenate(tu, 1)))
+                + dot_left((mat_h[0, 1], mat_h[1, 1]), halves(jnp.concatenate(tv, 1))))
 
     def inv_h(ps, first, last):
         vs = [spin(p) for p in ps]
-        g = (dot(mat_h[0], jnp.concatenate(ps, 1)) - dot(mat_h[1], jnp.concatenate(vs, 1))) * (1.0 / H)
+        g = (dot_left((mat_h[0, 0], mat_h[1, 0]), halves(jnp.concatenate(ps, 1)))
+             - dot_left((mat_h[0, 1], mat_h[1, 1]), halves(jnp.concatenate(vs, 1)))) * (1.0 / H)
         gu, gv = [], []
         for k1 in range(R):
             u = g[:, 2 * q * k1:2 * q * (k1 + 1)]
@@ -211,9 +228,7 @@
         for j in range(C):
             s1[k1 * C + j] = z[k1 * rows:(k1 + 1) * rows, 2 * q * j:2 * q * (j + 1)]
     x1.start()
-    x_k.start()
     r1[me16] = s1[me16]
-    k_recv[r] = k_send[r]
     x1.wait()
     x_k.wait()
 
@@ -325,19 +340,67 @@
     for j in range(C):
         s5[j] = adj[j]
     x5.start()
-    r5[c] = s5[c]
-    x5.wait()
+    down_d, down_r, down_c = lax.rem(d + D - 1, D), lax.rem(r + R - 1, R), lax.rem(c + C - 1, C)
+    far = d > 0
+
+    def plane_copy(t):
+        return rc(ups.at[t], h_dep.at[t], sm_dep.at[0, t], sm_dep.at[1, t], {"depth": d - 1})
+
+    def take(t, value):
+        ups[t] = vol[t] - step_size * value
+
+        @pl.when(far)
+        def _():
+            plane_copy(t).start()
+
+    take(c, s5[c])
+
+    def arrive(o):
+        t = lax.rem(c + o, C)
+        rc(s5.at[t], r5.at[t], sm5.at[0, t], sm5.at[1, t], col_dev(t)).wait()
+        take(t, r5[t])
+
+    loop(1, C, arrive)
     for j in range(C):
-        ups[j * rows:(j + 1) * rows, :] = vol[j] - step_size * r5[j]
-
-    down_d, down_r, down_c = lax.rem(d + D - 1, D), lax.rem(r + R - 1, R), lax.rem(c + C - 1, C)
+        edge[j * rows:(j + 1) * rows, :] = ups[j, :, 0:128]
     copies = [
-        rc(ups.at[0:8, :], h_row, sm_h.at[0, 1], sm_h.at[1, 1], {"row": down_r}),
-        rc(ups.at[:, 0:128], h_col, sm_h.at[0, 2], sm_h.at[1, 2], {"col": down_c}),
-        rc(ups, h_dep, sm_h.at[0, 0], sm_h.at[1, 0], {"depth": down_d}),
+        rc(ups.at[0, 0:8, :], h_row, sm_h.at[0, 0], sm_h.at[1, 0], {"row": down_r}),
+        rc(edge, h_col, sm_h.at[0, 1], sm_h.at[1, 1], {"col": down_c}),
     ]
     for cp in copies:
         cp.start()
+    for j in range(C):
+        out_u[j * rows:(j + 1) * rows, :] = ups[j]
+    copies[0].wait()
+    out_row[...] = h_row[...]
+    copies[1].wait()
+    out_col[...] = h_col[...]
+
+    @pl.when(far)
+    def _():
+        def sent(t):
+            plane_copy(t).wait_send()
+
+        loop(0, C, sent)
+
+    @pl.when(d < D - 1)
+    def _():
+        def landed(t):
+            rc(ups.at[t], h_dep.at[t], sm_dep.at[0, t], sm_dep.at[1, t], {"depth": d + 1}).wait_recv()
+
+        loop(0, C, landed)
+        for j in range(C):
+            out_dep[j * rows:(j + 1) * rows, :] = h_dep[j]
+
+    @pl.when(d == D - 1)
+    def _():
+        for j in range(C):
+            out_dep[j * rows:(j + 1) * rows, :] = ups[j]
+
+
+def tail(D, R, C, ups, dep, row, col, dual, upd, shr, dnx):
+    hb, wb = ups.shape
+    r, c = lax.axis_index("row"), lax.axis_index("col")
     u = ups[...]
     upd[0] = u
 
@@ -347,17 +410,18 @@
         shr[i, 0] = combined - clipped
         dnx[i, 0] = clipped
 
-    copies[0].wait()
+    finish(0, dep[...] - u)
     rid = lax.broadcasted_iota(jnp.int32, (hb, wb), 0)
-    nxt = jnp.where(rid == hb - 1, jnp.broadcast_to(h_row[0:1, :], (hb, wb)), pltpu.roll(u, hb - 1, 0))
-    finish(1, jnp.where(r * hb + rid < H - 1, nxt - u, 0.0))
-    copies[1].wait()
+    nxt = jnp.where(rid == hb - 1, jnp.broadcast_to(row[0:1, :], (hb, wb)), pltpu.roll(u, hb - 1, 0))
+    finish(1, jnp.where(r * hb + rid < hb * R - 1, nxt - u, 0.0))
     cid = lax.broadcasted_iota(jnp.int32, (hb, wb), 1)
-    nxt = jnp.where(cid == wb - 1, jnp.broadcast_to(h_col[:, 0:1], (hb, wb)), pltpu.roll(u, wb - 1, 1))
-    finish(2, jnp.where(c * wb + cid < W - 1, nxt - u, 0.0))
-    copies[2].wait()
-    live = (d + rid * 0) < D - 1
-    finish(0, jnp.where(live, h_dep[...] - u, 0.0))
+    nxt = jnp.where(cid == wb - 1, jnp.broadcast_to(col[:, 0:1], (hb, wb)), pltpu.roll(u, wb - 1, 1))
+    finish(2, jnp.where(c * wb + cid < wb * C - 1, nxt - u, 0.0))
+
+
+def two_halves(table):
+    high = table.astype(jnp.bfloat16)
+    return np.stack([high, (table - high.astype(np.float64)).astype(jnp.bfloat16)])
 
 
 def shards(D, R, C, volume, psf_spec, measured, dual):
@@ -371,10 +435,10 @@
     f = np.exp(-2j * np.pi * ((n2[:, None] * k2[None]) % wb) / wb).reshape(wb, C, 1, wb // C)
     top = np.concatenate([f.real, f.imag], 2).reshape(wb, 2 * wb)
     bot = np.concatenate([-f.imag, f.real], 2).reshape(wb, 2 * wb)
-    mat_w = np.concatenate([top, bot], 0).astype(np.float32)
+    mat_w = two_halves(np.concatenate([top, bot], 0))
     m = np.arange(hb)
     g = np.exp(-2j * np.pi * ((m[:, None] * m[None]) % hb) / hb)
-    mat_h = np.stack([g.real, g.imag]).astype(np.float32)
+    mat_h = two_halves(np.stack([g.real, g.imag]))
     t = np.exp(-2j * np.pi * (np.arange(C)[:, None] * n2[None]) / W)
     tw_w = np.stack([t.real, t.imag]).astype(np.float32)
     t = np.exp(-2j * np.pi * (m[:, None] * np.arange(R)[None]) / H)
@@ -383,16 +447,17 @@
     V = pltpu.VMEM
     dma = pltpu.SemaphoreType.DMA
     vm = pl.BlockSpec(memory_space=pltpu.VMEM)
-    return pl.pallas_call(
+    near = pl.pallas_call(
         functools.partial(body, D, R, C, hb, wb),
         name="admm",
         out_shape=(
-            jax.ShapeDtypeStruct((1, hb, wb), f32),
-            jax.ShapeDtypeStruct((3, 1, hb, wb), f32),
-            jax.ShapeDtypeStruct((3, 1, hb, wb), f32),
+            jax.ShapeDtypeStruct((hb, wb), f32),
+            jax.ShapeDtypeStruct((hb, wb), f32),
+            jax.ShapeDtypeStruct((8, wb), f32),
+            jax.ShapeDtypeStruct((hb, 128), f32),
         ),
-        in_specs=[vm] * 8,
-        out_specs=(vm, vm, vm),
+        in_specs=[vm] * 7,
+        out_specs=(vm, vm, vm, vm),
         scratch_shapes=[
             V((C, rows, wb), f32),
             V((R, hb, 2 * q), f32), V((R, hb, 2 * q), f32),
@@ -402,17 +467,29 @@
             V((n16, rs, 2 * q), f32), V((NO, rs, 2 * q), f32),
             V((n16, rows, 2 * q), f32), V((n16, rows, 2 * q), f32),
             V((C, rows, wb), f32), V((C, rows, wb), f32),
-            V((hb, wb), f32), V((hb, wb), f32), V((8, wb), f32), V((hb, 128), f32),
+            V((C, rows, wb), f32), V((C, rows, wb), f32), V((8, wb), f32), V((hb, 128), f32), V((hb, 128), f32),
             dma((2, C)), dma((2, R)), dma((2, C)), dma((2, n16)), dma((NO,)), dma((N,)),
-            dma((N,)), dma((NO,)), dma((2, n16)), dma((2, C)), dma((2, 3)),
+            dma((N,)), dma((NO,)), dma((2, n16)), dma((2, C)), dma((2, 2)), dma((2, C)),
         ],
         compiler_params=pltpu.CompilerParams(
             collective_id=0, has_side_effects=True, vmem_limit_bytes=60 * 1024 * 1024
         ),
     )(
-        volume.reshape(C, rows, wb), psf_spec.reshape(2, hb, wb), measured.reshape(C, D, rs, wb), dual,
+        volume.reshape(C, rows, wb), psf_spec.reshape(2, hb, wb), measured.reshape(C, D, rs, wb),
         jnp.asarray(mat_w), jnp.asarray(mat_h), jnp.asarray(tw_w), jnp.asarray(tw_h),
     )
+    return pl.pallas_call(
+        functools.partial(tail, D, R, C),
+        name="tail",
+        out_shape=(
+            jax.ShapeDtypeStruct((1, hb, wb), f32),
+            jax.ShapeDtypeStruct((3, 1, hb, wb), f32),
+            jax.ShapeDtypeStruct((3, 1, hb, wb), f32),
+        ),
+        in_specs=[vm] * 5,
+        out_specs=(vm, vm, vm),
+        compiler_params=pltpu.CompilerParams(vmem_limit_bytes=16 * 1024 * 1024),
+    )(*near, dual)
 
 
 def solution(mesh):

time: 88.8 us -> 85.1 us (0.958)
  Pallas kernels: 82.4 us -> 80.6 us
  local copies, waits for them, and re-layouts: 4.69 us -> 3.5 us
    pallas_call x1, Pallas kernels: 82.4 us -> 79.3 us  [shards(): pl.pallas_call(functools.partial(body, D, R, C, hb, wb), name='admm', out...]
    pallas_call x0 -> x1, Pallas kernels: none -> 1.36 us  [shards(): pl.pallas_call(functools.partial(tail, D, R, C), name='tail', out_shape=(...]
    unnamed x5 -> x10, local copies, waits for them, and re-layouts: 4.69 us -> 3.5 us
where the time goes in v2:
time: 85.1 us; the launch traced here: 84.8 us
  Pallas kernels  80.6 us (95%)
  local copies, waits for them, and re-layouts  3.5 us (4%)
    pallas_call x1, Pallas kernels, shards(): pl.pallas_call(functools.partial(body, D, R, C, hb, wb), name='admm', out...  79.3 us
    unnamed x10, local copies, waits for them, and re-layouts  3.5 us

profile of v2, /device:TPU:0, one launch (start us, length us, event | category | flops | bytes accessed | tf_op | source)
XLA Modules:
  0.0 84.8 jit_solution(16551010877390205969)
XLA Ops:
  0.6 0.0 copy-start
  0.6 79.3 %admm.1 = (f32[256,256]{1,0:T(8,128)}, f32[256,256]{1,0:T(8,128)}, f32[8,256]{1,0:T(8,128)}, f32[256,128]{1,0:T(8,128)}) custom-call(f32[4,64,256]{2,1,0:T(8,128)} %bitcast.4, f32[2,256,256]{2,1,0:T(8,128)} %bitcast.3, f32[4,2,32,256]{3,2,1,0:T(8,128)} %bitcast.5, bf16[2,512,512]{2,1,0:T(8,128)(2,1)} %constant.8.clone.mat_w, ...), custom_call_target="tpu_custom_call" | custom-call | tf_op jit(solution)/shard_map/admm/pallas_call | solution.py:450
  79.9 0.0 copy-done
  79.9 0.0 copy-start.1
  80.0 0.9 %copy-done.1 = f32[256,256]{1,0:T(8,128)S(1)} copy-done((f32[256,256]{1,0:T(8,128)S(1)}, f32[256,256]{1,0:T(8,128)}, u32[]{:S(2)}) %copy-start.1) | copy-done | bytes 262168
  80.9 0.0 copy-start.2
  80.9 0.9 %copy-done.2 = f32[256,256]{1,0:T(8,128)S(1)} copy-done((f32[256,256]{1,0:T(8,128)S(1)}, f32[256,256]{1,0:T(8,128)}, u32[]{:S(2)}) %copy-start.2) | copy-done | bytes 262168
  81.8 0.0 copy-start.3
  81.9 0.9 %copy-done.3 = f32[256,128]{1,0:T(8,128)S(1)} copy-done((f32[256,128]{1,0:T(8,128)S(1)}, f32[256,128]{1,0:T(8,128)}, u32[]{:S(2)}) %copy-start.3) | copy-done | bytes 131096
  82.8 0.0 copy-start.4
  82.8 0.7 copy-done.4
  83.5 1.4 %tail.1 = (f32[1,256,256]{2,1,0:T(8,128)}, f32[3,1,256,256]{3,2,1,0:T(8,128)}, f32[3,1,256,256]{3,2,1,0:T(8,128)}) custom-call(f32[256,256]{1,0:T(8,128)S(1)} %copy-done.1, f32[256,256]{1,0:T(8,128)S(1)} %copy-done.2, f32[8,256]{1,0:T(8,128)S(1)} %copy-done.4, f32[256,128]{1,0:T(8,128)S(1)} %copy-done.3, f32[3,1,256,256]{3,2,1,0:T(8,128)S(1)} %copy-done), custom_call_target="tpu_custom_call" | custom-call | tf_op jit(solution)/shard_map/tail/pallas_call | solution.py:481
Async XLA Ops:
  0.6 79.3 %copy-start = (f32[3,1,256,256]{3,2,1,0:T(8,128)S(1)}, f32[3,1,256,256]{3,2,1,0:T(8,128)}, u32[]{:S(2)}) copy-start(f32[3,1,256,256]{3,2,1,0:T(8,128)} %dual.1) | copy-start | bytes 2359300
  79.9 1.0 %copy-start.1 = (f32[256,256]{1,0:T(8,128)S(1)}, f32[256,256]{1,0:T(8,128)}, u32[]{:S(2)}) copy-start(f32[256,256]{1,0:T(8,128)} %get-tuple-element.7.ups) | copy-start | bytes 786436
  80.9 0.9 %copy-start.2 = (f32[256,256]{1,0:T(8,128)S(1)}, f32[256,256]{1,0:T(8,128)}, u32[]{:S(2)}) copy-start(f32[256,256]{1,0:T(8,128)} %get-tuple-element.8.dep) | copy-start | bytes 786436
  81.8 0.9 %copy-start.3 = (f32[256,128]{1,0:T(8,128)S(1)}, f32[256,128]{1,0:T(8,128)}, u32[]{:S(2)}) copy-start(f32[256,128]{1,0:T(8,128)} %get-tuple-element.10.col) | copy-start | bytes 393220
  82.8 0.7 copy-start.4

commit v3 on v2

--- a/solution.py
+++ b/solution.py
@@ -101,28 +101,37 @@
         def start(self):
             def go(o):
                 t = lax.rem(self.pos + o, self.n)
-                rc(self.src(t), self.recv.at[self.pos], self.sems.at[0, t], self.sems.at[1, self.pos], self.dev(t)).start()
+                rc(self.src(t), self.recv(self.pos), self.sems.at[0, t], self.sems.at[1, self.pos], self.dev(t)).start()
             loop(1, self.n, go)
 
         def wait(self):
             def go(o):
                 t = lax.rem(self.pos + o, self.n)
-                rc(self.src(t), self.recv.at[t], self.sems.at[0, t], self.sems.at[1, t], self.dev(t)).wait()
+                rc(self.src(t), self.recv(t), self.sems.at[0, t], self.sems.at[1, t], self.dev(t)).wait()
             loop(1, self.n, go)
 
     col_dev = lambda t: {"col": t}
     row_dev = lambda t: {"row": t}
     all_dev = lambda t: {"row": t // C, "col": lax.rem(t, C)}
 
-    x_vol = A2A(C, c, col_dev, lambda t: vol.at[t], r_vol, sm_vol)
-    x_k = A2A(R, r, row_dev, lambda t: k_send.at[t], k_recv, sm_k)
-    x_meas = A2A(C, c, col_dev, lambda t: meas.at[t, d], r_meas, sm_meas)
-    x1 = A2A(n16, me16, all_dev, lambda t: s1.at[t], r1, sm1)
-    x4 = A2A(n16, me16, all_dev, lambda t: s4.at[t], r4, sm4)
-    x5 = A2A(C, c, col_dev, lambda t: s5.at[t], r5, sm5)
+    half = rows // 2
+
+    def in_halves(n, pos, dev, send, recv, sems):
+        def one(h):
+            part = slice(h * half, (h + 1) * half)
+            return A2A(n, pos, dev, lambda t: send.at[t, part], lambda t: recv.at[t, part], sems.at[h])
+        return [one(0), one(1)]
+
+    x_vol = in_halves(C, c, col_dev, vol, r_vol, sm_vol)
+    x_k = A2A(R, r, row_dev, lambda t: k_send.at[t], lambda t: k_recv.at[t], sm_k)
+    x_meas = A2A(C, c, col_dev, lambda t: meas.at[t, d], lambda t: r_meas.at[t], sm_meas)
+    x1 = in_halves(n16, me16, all_dev, s1, r1, sm1)
+    x4 = in_halves(n16, me16, all_dev, s4, r4, sm4)
+    x5 = in_halves(C, c, col_dev, s5, r5, sm5)
 
     pl.semaphore_wait(barrier, N - 1)
-    x_vol.start()
+    x_vol[0].start()
+    x_vol[1].start()
     r_vol[c] = vol[c]
 
     kin = jnp.concatenate([psf[0], psf[1]], axis=1)
@@ -222,14 +231,17 @@
         lane = lax.broadcasted_iota(jnp.int32, k.shape, 1)
         return jnp.where(lane < q, k, rolled), jnp.where(lane < q, rolled, k)
 
-    x_vol.wait()
-    z = fwd_w([r_vol[j] for j in range(C)], 0)
-    for k1 in range(R):
-        for j in range(C):
-            s1[k1 * C + j] = z[k1 * rows:(k1 + 1) * rows, 2 * q * j:2 * q * (j + 1)]
-    x1.start()
+    for h in range(2):
+        part = slice(h * half, (h + 1) * half)
+        x_vol[h].wait()
+        z = fwd_w([r_vol[j, part] for j in range(C)], 0)
+        for k1 in range(R):
+            for j in range(C):
+                s1[k1 * C + j, part] = z[k1 * half:(k1 + 1) * half, 2 * q * j:2 * q * (j + 1)]
+        x1[h].start()
     r1[me16] = s1[me16]
-    x1.wait()
+    x1[0].wait()
+    x1[1].wait()
     x_k.wait()
 
     def joined(ref, first, count):
@@ -332,35 +344,42 @@
     for i in range(R):
         for j in range(C):
             s4[i * C + j] = xs[i][j * rows:(j + 1) * rows, :]
-    x4.start()
+    x4[0].start()
+    x4[1].start()
     r4[me16] = s4[me16]
-    x4.wait()
-    zs = [jnp.concatenate([r4[k1 * C + j] for j in range(C)], 1) for k1 in range(R)]
-    adj = inv_w(jnp.concatenate(zs, 0), rows, 0, C)
-    for j in range(C):
-        s5[j] = adj[j]
-    x5.start()
+    for h in range(2):
+        part = slice(h * half, (h + 1) * half)
+        x4[h].wait()
+        zs = [jnp.concatenate([r4[k1 * C + j, part] for j in range(C)], 1) for k1 in range(R)]
+        adj = inv_w(jnp.concatenate(zs, 0), half, 0, C)
+        for j in range(C):
+            s5[j, part] = adj[j]
+        x5[h].start()
     down_d, down_r, down_c = lax.rem(d + D - 1, D), lax.rem(r + R - 1, R), lax.rem(c + C - 1, C)
     far = d > 0
 
-    def plane_copy(t):
-        return rc(ups.at[t], h_dep.at[t], sm_dep.at[0, t], sm_dep.at[1, t], {"depth": d - 1})
-
-    def take(t, value):
-        ups[t] = vol[t] - step_size * value
-
-        @pl.when(far)
-        def _():
-            plane_copy(t).start()
-
-    take(c, s5[c])
-
-    def arrive(o):
-        t = lax.rem(c + o, C)
-        rc(s5.at[t], r5.at[t], sm5.at[0, t], sm5.at[1, t], col_dev(t)).wait()
-        take(t, r5[t])
-
-    loop(1, C, arrive)
+    def plane_copy(t, h, to):
+        part = slice(h * half, (h + 1) * half)
+        return rc(ups.at[t, part], h_dep.at[t, part], sm_dep.at[h, 0, t], sm_dep.at[h, 1, t], {"depth": to})
+
+    for h in range(2):
+        part = slice(h * half, (h + 1) * half)
+
+        def take(t, value):
+            ups[t, part] = vol[t, part] - step_size * value
+
+            @pl.when(far)
+            def _():
+                plane_copy(t, h, d - 1).start()
+
+        take(c, s5[c, part])
+
+        def arrive(o):
+            t = lax.rem(c + o, C)
+            rc(s5.at[t, part], r5.at[t, part], sm5.at[h, 0, t], sm5.at[h, 1, t], col_dev(t)).wait()
+            take(t, r5[t, part])
+
+        loop(1, C, arrive)
     for j in range(C):
         edge[j * rows:(j + 1) * rows, :] = ups[j, :, 0:128]
     copies = [
@@ -379,14 +398,16 @@
     @pl.when(far)
     def _():
         def sent(t):
-            plane_copy(t).wait_send()
+            plane_copy(t, 0, d - 1).wait_send()
+            plane_copy(t, 1, d - 1).wait_send()
 
         loop(0, C, sent)
 
     @pl.when(d < D - 1)
     def _():
         def landed(t):
-            rc(ups.at[t], h_dep.at[t], sm_dep.at[0, t], sm_dep.at[1, t], {"depth": d + 1}).wait_recv()
+            plane_copy(t, 0, d + 1).wait_recv()
+            plane_copy(t, 1, d + 1).wait_recv()
 
         loop(0, C, landed)
         for j in range(C):
@@ -468,8 +489,8 @@
             V((n16, rows, 2 * q), f32), V((n16, rows, 2 * q), f32),
             V((C, rows, wb), f32), V((C, rows, wb), f32),
             V((C, rows, wb), f32), V((C, rows, wb), f32), V((8, wb), f32), V((hb, 128), f32), V((hb, 128), f32),
-            dma((2, C)), dma((2, R)), dma((2, C)), dma((2, n16)), dma((NO,)), dma((N,)),
-            dma((N,)), dma((NO,)), dma((2, n16)), dma((2, C)), dma((2, 2)), dma((2, C)),
+            dma((2, 2, C)), dma((2, R)), dma((2, C)), dma((2, 2, n16)), dma((NO,)), dma((N,)),
+            dma((N,)), dma((NO,)), dma((2, 2, n16)), dma((2, 2, C)), dma((2, 2)), dma((2, 2, C)),
         ],
         compiler_params=pltpu.CompilerParams(
             collective_id=0, has_side_effects=True, vmem_limit_bytes=60 * 1024 * 1024
@@ -488,7 +509,7 @@
         ),
         in_specs=[vm] * 5,
         out_specs=(vm, vm, vm),
-        compiler_params=pltpu.CompilerParams(vmem_limit_bytes=16 * 1024 * 1024),
+        compiler_params=pltpu.CompilerParams(vmem_limit_bytes=60 * 1024 * 1024),
     )(*near, dual)
 
 

time: 85.1 us -> 82.7 us (0.972)
  local copies, waits for them, and re-layouts: 3.5 us -> 0 us
  Pallas kernels: 80.6 us -> 81.8 us
    unnamed x10 -> x0, local copies, waits for them, and re-layouts: 3.5 us -> none
    pallas_call x1, Pallas kernels: 1.36 us -> 2.74 us  [shards(): pl.pallas_call(functools.partial(tail, D, R, C), name='tail', out_shape=(...]
where the time goes in v3:
time: 82.7 us; the launch traced here: 82.5 us
  Pallas kernels  81.8 us (99%)
    pallas_call x1, Pallas kernels, shards(): pl.pallas_call(functools.partial(body, D, R, C, hb, wb), name='admm', out...  79.1 us
    pallas_call x1, Pallas kernels, shards(): pl.pallas_call(functools.partial(tail, D, R, C), name='tail', out_shape=(...  2.74 us

profile of v3, /device:TPU:0, one launch (start us, length us, event | category | flops | bytes accessed | tf_op | source)
XLA Modules:
  0.0 82.5 jit_solution(9629370132429186039)
XLA Ops:
  0.6 79.1 %admm.1 = (f32[256,256]{1,0:T(8,128)}, f32[256,256]{1,0:T(8,128)}, f32[8,256]{1,0:T(8,128)}, f32[256,128]{1,0:T(8,128)}) custom-call(f32[4,64,256]{2,1,0:T(8,128)} %bitcast.4, f32[2,256,256]{2,1,0:T(8,128)} %bitcast.3, f32[4,2,32,256]{3,2,1,0:T(8,128)} %bitcast.5, bf16[2,512,512]{2,1,0:T(8,128)(2,1)} %constant.8.clone.mat_w, ...), custom_call_target="tpu_custom_call" | custom-call | tf_op jit(solution)/shard_map/admm/pallas_call | solution.py:471
  79.8 2.7 %tail.1 = (f32[1,256,256]{2,1,0:T(8,128)}, f32[3,1,256,256]{3,2,1,0:T(8,128)}, f32[3,1,256,256]{3,2,1,0:T(8,128)}) custom-call(f32[256,256]{1,0:T(8,128)} %get-tuple-element.7.ups, f32[256,256]{1,0:T(8,128)} %get-tuple-element.8.dep, f32[8,256]{1,0:T(8,128)} %get-tuple-element.9.row, f32[256,128]{1,0:T(8,128)} %get-tuple-element.10.col, f32[3,1,256,256]{3,2,1,0:T(8,128)} %dual.1), custom_call_target="tpu_custom_call" | custom-call | tf_op jit(solution)/shard_map/tail/pallas_call | solution.py:502

commit v4 on v3

--- a/solution.py
+++ b/solution.py
@@ -94,6 +94,9 @@
             return x
         lax.fori_loop(lower, upper, g, 0)
 
+    far_cols = sorted(range(C), key=lambda k: (k == 0, abs(k - C // 2)))
+    far_first = [(co, ro) for co in far_cols for ro in range(R)]
+
     class A2A:
         def __init__(self, n, pos, dev, src, recv, sems):
             self.n, self.pos, self.dev, self.src, self.recv, self.sems = n, pos, dev, src, recv, sems
@@ -102,7 +105,13 @@
             def go(o):
                 t = lax.rem(self.pos + o, self.n)
                 rc(self.src(t), self.recv(self.pos), self.sems.at[0, t], self.sems.at[1, self.pos], self.dev(t)).start()
-            loop(1, self.n, go)
+            if self.n == R:
+                loop(1, self.n, go)
+                return
+            for co, ro in far_first:
+                t = lax.rem(r + ro, R) * C + lax.rem(c + co, C)
+                if (co, ro) != (0, 0):
+                    rc(self.src(t), self.recv(self.pos), self.sems.at[0, t], self.sems.at[1, self.pos], self.dev(t)).start()
 
         def wait(self):
             def go(o):
@@ -263,8 +272,8 @@
     def owner_id(t):
         return (t // (NR * C)) * n16 + (lo + (t // C) % NR) * C + t % C
 
-    def send2(o):
-        t = lax.rem(me + o, NO)
+    def send2(o, co):
+        t = lax.rem(d * NR + r + o, D * NR) * C + lax.rem(c + co, C)
         w = owner_id(t)
 
         @pl.when(w != me)
@@ -275,7 +284,8 @@
         def _():
             r2[me] = s2[t]
 
-    loop(0, NO, send2)
+    for co in far_cols:
+        loop(0, D * NR, functools.partial(send2, co=co))
     x_meas.wait()
     is_owner = (r >= lo) & (r < hi)
     my_owner = ((r - lo) * C + c) * D + d
@@ -303,11 +313,12 @@
             for j in range(C):
                 s3[k1 * C + j] = zz[k1 * rs:(k1 + 1) * rs, 2 * q * j:2 * q * (j + 1)]
 
-        def send3(o):
-            t = lax.rem(me + o, N)
+        def send3(o, co, ro):
+            t = lax.rem(d + o, D) * n16 + lax.rem(r + ro, R) * C + lax.rem(c + co, C)
             rc(s3.at[lax.rem(t, n16)], r3.at[my_owner], sm3s.at[t], sm3r.at[my_owner], ids(t)).start()
 
-        loop(1, N, send3)
+        for co, ro in far_first:
+            loop(1 if (co, ro) == (0, 0) else 0, D, functools.partial(send3, co=co, ro=ro))
         r3[my_owner] = s3[me16]
 
         def drain3(o):

time: 82.7 us -> 82.2 us (level)
  no operation moved by 1% of the time
where the time goes in v4:
time: 82.2 us; the launch traced here: 82 us
  Pallas kernels  81.4 us (99%)
    pallas_call x1, Pallas kernels, shards(): pl.pallas_call(functools.partial(body, D, R, C, hb, wb), name='admm', out...  78.6 us
    pallas_call x1, Pallas kernels, shards(): pl.pallas_call(functools.partial(tail, D, R, C), name='tail', out_shape=(...  2.74 us

profile of v4, /device:TPU:0, one launch (start us, length us, event | category | flops | bytes accessed | tf_op | source)
XLA Modules:
  0.0 82.0 jit_solution(4612470490949344999)
XLA Ops:
  0.6 78.6 %admm.1 = (f32[256,256]{1,0:T(8,128)}, f32[256,256]{1,0:T(8,128)}, f32[8,256]{1,0:T(8,128)}, f32[256,128]{1,0:T(8,128)}) custom-call(f32[4,64,256]{2,1,0:T(8,128)} %bitcast.4, f32[2,256,256]{2,1,0:T(8,128)} %bitcast.3, f32[4,2,32,256]{3,2,1,0:T(8,128)} %bitcast.5, bf16[2,512,512]{2,1,0:T(8,128)(2,1)} %constant.8.clone.mat_w, ...), custom_call_target="tpu_custom_call" | custom-call | tf_op jit(solution)/shard_map/admm/pallas_call | solution.py:482
  79.3 2.7 %tail.1 = (f32[1,256,256]{2,1,0:T(8,128)}, f32[3,1,256,256]{3,2,1,0:T(8,128)}, f32[3,1,256,256]{3,2,1,0:T(8,128)}) custom-call(f32[256,256]{1,0:T(8,128)} %get-tuple-element.7.ups, f32[256,256]{1,0:T(8,128)} %get-tuple-element.8.dep, f32[8,256]{1,0:T(8,128)} %get-tuple-element.9.row, f32[256,128]{1,0:T(8,128)} %get-tuple-element.10.col, f32[3,1,256,256]{3,2,1,0:T(8,128)} %dual.1), custom_call_target="tpu_custom_call" | custom-call | tf_op jit(solution)/shard_map/tail/pallas_call | solution.py:513
